TPU v7x, 32 devices: a whole 2x2x4 slice. The times are simulated.
32 devices in a mesh: chan: 4 (over x, core), rad: 8 (over z, y).
Axes of the slice: x: 2, y: 2, z: 4, core: 2. Of those that a mesh axis runs over, the one named last changes fastest.
Arguments:
- psi: float32 [2, 768, 128, 128], P(None, 'chan', 'rad'), may hold values from -6 to 6
- k_prev: float32 [2, 768, 128, 128], P(None, 'chan', 'rad'), may hold values from -6 to 6
- gaunt: bfloat16 [4, 768, 768], replicated, may hold values from -0.875 to 0.875
- dipole: bfloat16 [768, 768], replicated, may hold values from -0.875 to 0.875
- kinetic: float32 [128, 128], replicated, as said below
- chan_l: int32 [768, 2], P('chan'), may hold values from 0 to 23
- field_amp: float32 [1], replicated, may hold values from 0.02 to 0.1
Outputs:
- deriv: float32 [2, 768, 128, 128], P(None, 'chan', 'rad')
Inputs may be any that keep to these rules, and one draw needn't show every extreme that they name: `kinetic`: symmetric; zero where the row's and the column's blocks of 16 indices are more than one block apart.
All inputs are finite; a program needn't handle non-finite values.
Results may differ from a plain program's by a relative error of at most 0.00037.
Values may be sent and summed in bfloat16 or wider, within the bound.
A program may use at most 64 MiB of HBM per device.

v0:
```python
import jax
import jax.numpy as jnp
from jax import lax
from jax.sharding import PartitionSpec as P


def extended(array, sides, width):
    for axis, dim in sides:
        peers, length = (lax.axis_size(axis), array.shape[dim])
        up = [(i, (i + 1) % peers) for i in range(peers - 1)]
        down = [(j, i) for i, j in up]
        last = lax.slice_in_dim(array, length - width, length, axis=dim)
        initial = lax.slice_in_dim(array, 0, width, axis=dim)
        before = lax.ppermute(last, axis, up)
        after = lax.ppermute(initial, axis, down)
        array = jnp.concatenate([before, array, after], axis=dim)
    return array


def on_device(psi, k_prev, gaunt, dipole, kinetic, chan_l, field_amp):
    highest = lax.Precision.HIGHEST
    section = psi + 0.5 * k_prev
    local_chan = section.shape[1]
    rows = section.shape[2]
    width = section.shape[3]
    rad_at = lax.axis_index("rad")
    first_r = (
        1.0 + 8.0 * (rad_at * rows + jnp.arange(rows, dtype=jnp.int32)).astype(jnp.float32) / width
    )
    second_r = 1.0 + 8.0 * jnp.arange(width, dtype=jnp.float32) / width
    along_r2 = jnp.einsum("acij,kj->acik", section, kinetic, precision=highest)
    padded = extended(section.astype(jnp.bfloat16), (("rad", 2),), rows).astype(section.dtype)
    band = lax.dynamic_slice_in_dim(kinetic, rad_at * rows, rows, 0)
    widened = jnp.pad(band, ((0, 0), (rows, rows)))
    local_band = lax.dynamic_slice_in_dim(widened, rad_at * rows, 3 * rows, 1)
    along_r1 = jnp.einsum("ij,acjk->acik", local_band, padded, precision=highest)
    lvals = chan_l.astype(jnp.float32)
    first_l = lvals[:, 0] * (lvals[:, 0] + 1.0)
    second_l = lvals[:, 1] * (lvals[:, 1] + 1.0)
    potential = (
        first_l[:, None, None] / (2.0 * first_r * first_r)[None, :, None]
        + second_l[:, None, None] / (2.0 * second_r * second_r)[None, None, :]
        - 2.0 / first_r[None, :, None]
        - 2.0 / second_r[None, None, :]
    )
    sent = section.astype(jnp.bfloat16).reshape(2, local_chan, rows * width)
    chan_at = lax.axis_index("chan")
    block = lax.all_to_all(sent, "chan", split_axis=2, concat_axis=1, tiled=True)
    count = block.shape[2]
    place = chan_at * count + jnp.arange(count, dtype=jnp.int32)
    row_r = 1.0 + 8.0 * (rad_at * rows + place // width).astype(jnp.float32) / width
    col_r = 1.0 + 8.0 * (place % width).astype(jnp.float32) / width
    far = jnp.maximum(row_r, col_r)
    near = jnp.minimum(row_r, col_r)
    inverse = 1.0 / far
    ratio = near * inverse
    power = inverse
    total = jnp.zeros(block.shape, jnp.float32)
    for order in range(gaunt.shape[0]):
        mixed = jnp.einsum("cd,adq->acq", gaunt[order], block, preferred_element_type=jnp.float32)
        total = total + power[None, None, :] * mixed
        power = power * ratio
    mixed = jnp.einsum("cd,adq->acq", dipole, block, preferred_element_type=jnp.float32)
    total = total + (field_amp[0] * (row_r + col_r))[None, None, :] * mixed
    coupled = lax.all_to_all(
        total.astype(jnp.bfloat16), "chan", split_axis=1, concat_axis=2, tiled=True
    )
    coupled = coupled.reshape(coupled.shape[0], local_chan, rows, width)
    ham = along_r1 + along_r2 + potential[None] * section + coupled.astype(jnp.float32)
    return jnp.stack([ham[1], -ham[0]])


def solution(mesh):
    placed = (
        P(None, "chan", "rad", None),
        P(None, "chan", "rad", None),
        P(),
        P(),
        P(),
        P("chan", None),
        P(),
    )
    return jax.shard_map(
        on_device,
        mesh=mesh,
        in_specs=placed,
        out_specs=P(None, "chan", "rad", None),
        check_vma=False,
    )
```

profile of v0, /device:TPU:0, one launch (start us, length us, event | category | flops | bytes accessed | tf_op | source)
XLA Modules:
  0.0 111.4 jit_solution(17644316627872621807)
XLA Ops:
  0.0 4.5 %fusion.45 = bf16[2,192,16,128]{3,2,1,0:T(8,128)(2,1)} fusion(f32[2,192,16,128]{3,2,1,0:T(8,128)} %param.7, f32[2,192,16,128]{3,2,1,0:T(8,128)} %param.8), kind=kLoop, calls=%fused_computation.70 | loop fusion | flops 2359296 | bytes 7864320 | tf_op jit(solution)/shard_map/convert_element_type | solution.py:32
  4.5 6.2 %collective-permute-start = (bf16[2,192,16,128]{3,2,1,0:T(8,128)(2,1)}, bf16[2,192,16,128]{3,2,1,0:T(8,128)(2,1)}, u32[]{:S(2)}, u32[]{:S(2)}) collective-permute-start(bf16[2,192,16,128]{3,2,1,0:T(8,128)(2,1)} %fusion.45), channel_id=1, source_target_pairs={{0,1},{1,2},{2,3},{3,4},{4,5},{5,6},{6,7},{8,9},{9,10},{10,11},{11... | collective-permute-start | bytes 4718600 | tf_op jit(solution)/shard_map/ppermute | solution.py:14
  10.7 1.3 %collective-permute-start.1 = (bf16[2,192,16,128]{3,2,1,0:T(8,128)(2,1)}, bf16[2,192,16,128]{3,2,1,0:T(8,128)(2,1)}, u32[]{:S(2)}, u32[]{:S(2)}) collective-permute-start(bf16[2,192,16,128]{3,2,1,0:T(8,128)(2,1)} %fusion.45), channel_id=1, source_target_pairs={{1,0},{2,1},{3,2},{4,3},{5,4},{6,5},{7,6},{9,8},{10,9},{11,10},{12... | collective-permute-start | bytes 4718600 | tf_op jit(solution)/shard_map/ppermute | solution.py:15
  12.0 4.6 %copy.43 = bf16[2,192,16,128]{1,0,3,2:T(2,128)(2,1)} copy(bf16[2,192,16,128]{3,2,1,0:T(8,128)(2,1)} %fusion.45) | data formatting | bytes 3145728 | tf_op jit(solution)/shard_map/reshape | solution.py:46
  16.6 3.6 %all-to-all-start = ((bf16[2,192,2048]{1,0,2:T(2,128)(2,1)}), bf16[2,192,2048]{1,0,2:T(2,128)(2,1)S(1)}, u32[]{:S(2)}, u32[]{:S(2)}) async-start(bf16[2,192,2048]{1,0,2:T(2,128)(2,1)} %bitcast.55), calls=%async_computation | async-start | bytes 4194304 | tf_op jit(solution)/shard_map/all_to_all | solution.py:48
  21.2 24.7 %all-to-all-done = bf16[2,192,2048]{1,0,2:T(2,128)(2,1)S(1)} async-done(((bf16[2,192,2048]{1,0,2:T(2,128)(2,1)}), bf16[2,192,2048]{1,0,2:T(2,128)(2,1)S(1)}, u32[]{:S(2)}, u32[]{:S(2)}) %all-to-all-start) | async-done | bytes 1572896 | tf_op jit(solution)/shard_map/all_to_all | solution.py:48
  45.8 4.6 %copy.44 = bf16[2,192,4,512]{3,2,1,0:T(4,128)(2,1)} copy(bf16[2,192,4,512]{1,0,3,2:T(2,128)(2,1)S(1)} %bitcast.54) | data formatting | bytes 3145728 | tf_op jit(solution)/shard_map/all_to_all | solution.py:48
  50.5 1.9 %copy.27 = bf16[2,4,192,512]{3,2,1,0:T(8,128)(2,1)S(1)} copy(bf16[2,4,192,512]{3,1,2,0:T(4,128)(2,1)} %bitcast.56) | data formatting | bytes 3145728 | tf_op jit(solution)/shard_map/all_to_all | solution.py:48
  52.4 2.8 %fusion.12 = f32[2,512,768]{2,1,0:T(8,128)S(1)} fusion(bf16[2,768,512]{2,1,0:T(8,128)(2,1)S(1)} %bitcast.58, bf16[4,768,768]{2,1,0:T(8,128)(2,1)} %param.9), kind=kOutput, calls=%fused_computation.17 | convolution fusion | flops 1207959552 | bytes 5898240 | tf_op jit(solution)/shard_map/cd,adq->acq/dot_general | solution.py:60
  55.1 2.7 %fusion.14 = f32[2,512,768]{2,1,0:T(8,128)S(1)} fusion(bf16[2,768,512]{2,1,0:T(8,128)(2,1)S(1)} %bitcast.59, bf16[4,768,768]{2,1,0:T(8,128)(2,1)} %param.9), kind=kOutput, calls=%fused_computation.19 | convolution fusion | flops 1207959552 | bytes 5898240 | tf_op jit(solution)/shard_map/cd,adq->acq/dot_general | solution.py:60
  57.9 1.4 %fusion.16 = f32[2,512,768]{2,1,0:T(8,128)S(1)} fusion(bf16[2,768,512]{2,1,0:T(8,128)(2,1)S(1)} %bitcast.60, bf16[4,768,768]{2,1,0:T(8,128)(2,1)S(1)} %bitcast.66), kind=kOutput, calls=%fused_computation.21 | convolution fusion | flops 1207959552 | bytes 5898240 | tf_op jit(solution)/shard_map/cd,adq->acq/dot_general | solution.py:60
  59.3 1.4 %fusion.18 = f32[2,512,768]{2,1,0:T(8,128)S(1)} fusion(bf16[2,768,512]{2,1,0:T(8,128)(2,1)S(1)} %bitcast.61, bf16[4,768,768]{2,1,0:T(8,128)(2,1)S(1)} %bitcast.66), kind=kOutput, calls=%fused_computation.23 | convolution fusion | flops 1207959552 | bytes 5898240 | tf_op jit(solution)/shard_map/cd,adq->acq/dot_general | solution.py:60
  60.8 2.7 %fusion.10 = bf16[2,768,512]{1,2,0:T(8,128)(2,1)S(1)} fusion(bf16[2,768,512]{2,1,0:T(8,128)(2,1)S(1)} %bitcast.62, f32[512]{0:T(512)S(1)} %get-tuple-element.9, f32[2,512,768]{2,1,0:T(8,128)S(1)} %fusion.12, f32[512]{0:T(512)S(1)} %get-tuple-element.12, f32[2,512,768]{2,1,0:T(8,128)S(1)} %fusion.14, f32[512]{0:T(512)S(1)} %fusion.40, ...), kind=kOutput, calls=%fused_computation.15 | convolution fusion | flops 1215823872 | bytes 16918528 | tf_op jit(solution)/shard_map/cd,adq->acq/dot_general | solution.py:63
  63.4 3.0 %copy.33 = bf16[2,768,512]{2,0,1:T(2,128)(2,1)} copy(bf16[2,768,512]{1,2,0:T(8,128)(2,1)S(1)} %fusion.10) | data formatting | bytes 3145728 | tf_op jit(solution)/shard_map/convert_element_type | solution.py:66
  66.5 4.5 %all-to-all-start.1 = ((bf16[2,768,512]{2,0,1:T(2,128)(2,1)}), bf16[2,768,512]{2,0,1:T(2,128)(2,1)}, u32[]{:S(2)}, u32[]{:S(2)}) async-start(bf16[2,768,512]{2,0,1:T(2,128)(2,1)} %copy.33), calls=%async_computation.1 | async-start | bytes 3145728 | tf_op jit(solution)/shard_map/all_to_all | solution.py:65
  71.1 0.5 subtract_subtract_fusion
  71.6 5.9 %fusion.24 = f32[2,192,16,128]{3,2,1,0:T(8,128)} fusion(f32[128,128]{1,0:T(8,128)S(1)} %copy-done.1, f32[2,192,16,128]{3,2,1,0:T(8,128)} %param.7, f32[2,192,16,128]{3,2,1,0:T(8,128)} %param.8), kind=kOutput, calls=%fused_computation.29 | convolution fusion | flops 1209532416 | bytes 9502720 | tf_op jit(solution)/shard_map/acij,kj->acik/dot_general | solution.py:31
  77.5 13.5 %all-to-all-done.1 = bf16[2,768,512]{2,0,1:T(2,128)(2,1)} async-done(((bf16[2,768,512]{2,0,1:T(2,128)(2,1)}), bf16[2,768,512]{2,0,1:T(2,128)(2,1)}, u32[]{:S(2)}, u32[]{:S(2)}) %all-to-all-start.1) | async-done | bytes 1572896 | tf_op jit(solution)/shard_map/all_to_all | solution.py:65
  90.9 1.7 %copy.34 = bf16[2,768,512]{2,1,0:T(8,128)(2,1)S(1)} copy(bf16[2,768,512]{2,0,1:T(2,128)(2,1)} %all-to-all-done.1) | data formatting | bytes 3145728 | tf_op jit(solution)/shard_map/all_to_all | solution.py:65
  92.6 0.4 convert_bitcast_fusion
  93.0 3.7 %copy.35 = f32[2,192,4,512]{3,2,1,0:T(4,128)} copy(f32[2,192,4,512]{3,1,2,0:T(8,128)S(1)} %convert_bitcast_fusion) | data formatting | bytes 6291456 | tf_op jit(solution)/shard_map/convert_element_type | solution.py:69
  96.7 5.1 %reshape.171 = f32[2,192,16,128]{3,2,1,0:T(8,128)} reshape(f32[2,192,4,512]{3,2,1,0:T(4,128)} %copy.35) | data formatting | bytes 6291456 | tf_op jit(solution)/shard_map/convert_element_type | solution.py:69
  101.8 7.6 %fusion.7 = f32[2,192,16,128]{3,2,1,0:T(8,128)S(1)} fusion(f32[2,192,16,128]{3,2,1,0:T(8,128)} %reshape.171, f32[2,192,16,128]{3,2,1,0:T(8,128)} %fusion.24, bf16[2,192,16,128]{3,2,1,0:T(8,128)(2,1)} %collective-permute-done.1, bf16[2,192,16,128]{3,2,1,0:T(8,128)(2,1)} %fusion.45, bf16[2,192,16,128]{3,2,1,0:T(8,128)(2,1)} %collective-permute-done, ...), kind=kOutput, calls=%fused_computation.10 | convolution fusion | flops 471859200 | bytes 22028292 | tf_op jit(solution)/shard_map/ij,acjk->acik/dot_general | solution.py:36
  109.7 1.7 %copy-done.4 = f32[2,192,16,128]{3,2,1,0:T(8,128)} copy-done((f32[2,192,16,128]{3,2,1,0:T(8,128)}, f32[2,192,16,128]{3,2,1,0:T(8,128)S(1)}, u32[]{:S(2)}) %copy-start.4) | copy-done | bytes 3145752
  (32 shorter events, 0.6 us)
Async XLA Ops:
  0.0 60.8 %copy-start = (bf16[768,768]{1,0:T(8,128)(2,1)S(1)}, bf16[768,768]{1,0:T(8,128)(2,1)}, u32[]{:S(2)}) copy-start(bf16[768,768]{1,0:T(8,128)(2,1)} %param.10) | copy-start | bytes 3538948
  4.5 16.4 %copy-start.2 = (s32[192,2]{0,1:T(2,128)S(1)}, s32[192,2]{0,1:T(2,128)}, u32[]{:S(2)}) copy-start(s32[192,2]{0,1:T(2,128)} %param.12) | copy-start | bytes 4612
  4.5 16.5 %copy-start.1 = (f32[128,128]{1,0:T(8,128)S(1)}, f32[128,128]{1,0:T(8,128)}, u32[]{:S(2)}) copy-start(f32[128,128]{1,0:T(8,128)} %param.11) | copy-start | bytes 196612
  4.5 97.3 %collective-permute-start = (bf16[2,192,16,128]{3,2,1,0:T(8,128)(2,1)}, bf16[2,192,16,128]{3,2,1,0:T(8,128)(2,1)}, u32[]{:S(2)}, u32[]{:S(2)}) collective-permute-start(bf16[2,192,16,128]{3,2,1,0:T(8,128)(2,1)} %fusion.45), channel_id=1, source_target_pairs={{0,1},{1,2},{2,3},{3,4},{4,5},{5,6},{6,7},{8,9},{9,10},{10,11},{11... | collective-permute-start | bytes 4718600 | tf_op jit(solution)/shard_map/ppermute | solution.py:14
  10.7 91.1 %collective-permute-start.1 = (bf16[2,192,16,128]{3,2,1,0:T(8,128)(2,1)}, bf16[2,192,16,128]{3,2,1,0:T(8,128)(2,1)}, u32[]{:S(2)}, u32[]{:S(2)}) collective-permute-start(bf16[2,192,16,128]{3,2,1,0:T(8,128)(2,1)} %fusion.45), channel_id=1, source_target_pairs={{1,0},{2,1},{3,2},{4,3},{5,4},{6,5},{7,6},{9,8},{10,9},{11,10},{12... | collective-permute-start | bytes 4718600 | tf_op jit(solution)/shard_map/ppermute | solution.py:15
  16.6 29.2 %all-to-all-start = ((bf16[2,192,2048]{1,0,2:T(2,128)(2,1)}), bf16[2,192,2048]{1,0,2:T(2,128)(2,1)S(1)}, u32[]{:S(2)}, u32[]{:S(2)}) async-start(bf16[2,192,2048]{1,0,2:T(2,128)(2,1)} %bitcast.55), calls=%async_computation | async-start | bytes 4194304 | tf_op jit(solution)/shard_map/all_to_all | solution.py:48
  50.5 7.4 %slice-start = ((s8[4718592]{0:T(1024)(128)(4,1)}), s8[4194304]{0:T(1024)(128)(4,1)S(1)}, s32[]{:S(2)}) async-start(s8[4718592]{0:T(1024)(128)(4,1)} %bitcast.65), calls=%async_computation.2 | async-start | bytes 8388608
  52.4 5.5 %slice-start.1 = ((s8[4718592]{0:T(1024)(128)(4,1)}), s8[524288]{0:T(1024)(128)(4,1)S(1)}, s32[]{:S(2)}) async-start(s8[4718592]{0:T(1024)(128)(4,1)} %bitcast.65), calls=%async_computation.3 | async-start | bytes 1048576
  66.5 24.5 %all-to-all-start.1 = ((bf16[2,768,512]{2,0,1:T(2,128)(2,1)}), bf16[2,768,512]{2,0,1:T(2,128)(2,1)}, u32[]{:S(2)}, u32[]{:S(2)}) async-start(bf16[2,768,512]{2,0,1:T(2,128)(2,1)} %copy.33), calls=%async_computation.1 | async-start | bytes 3145728 | tf_op jit(solution)/shard_map/all_to_all | solution.py:65
  101.8 7.6 %copy-start.3 = (f32[2,192,16,128]{3,2,1,0:T(8,128)S(1)}, f32[2,192,16,128]{3,2,1,0:T(8,128)}, u32[]{:S(2)}) copy-start(f32[2,192,16,128]{3,2,1,0:T(8,128)} %custom-call) | copy-start | bytes 9437188
  109.7 1.7 %copy-start.4 = (f32[2,192,16,128]{3,2,1,0:T(8,128)}, f32[2,192,16,128]{3,2,1,0:T(8,128)S(1)}, u32[]{:S(2)}) copy-start(f32[2,192,16,128]{3,2,1,0:T(8,128)S(1)} %get-tuple-element.17) | copy-start | bytes 9437188
where the time goes:
time: 112 us; the launch traced here: 111 us
  waiting for transfers between devices  38.1 us (34%)
  local copies, waits for them, and re-layouts  26.3 us (23%)
  matrix products  24.4 us (22%)
  starting transfers between devices  15.6 us (14%)
  other arithmetic  5.95 us (5%)
    all_to_all x1, waiting for transfers between devices, on_device(): lax.all_to_all(sent, 'chan', split_axis=2, concat_axis=1, tiled=True)  24.7 us
    all_to_all x1, waiting for transfers between devices, on_device(): lax.all_to_all(total.astype(jnp.bfloat16), 'chan', split_axis=1, concat_a...  13.5 us
    convert_element_type x2, local copies, waits for them, and re-layouts, on_device(): coupled.astype(jnp.float32)  8.79 us
    dot_general x4, matrix products, on_device(): jnp.einsum('cd,adq->acq', gaunt[order], block, preferred_element_type=jnp...  8.34 us
    dot_general x1, matrix products, on_device(): jnp.einsum('ij,acjk->acik', local_band, padded, precision=highest)  7.55 us
    all_to_all x2, local copies, waits for them, and re-layouts, on_device(): lax.all_to_all(sent, 'chan', split_axis=2, concat_axis=1, tiled=True)  6.5 us
    ppermute x1, starting transfers between devices, extended(): before = lax.ppermute(last, axis, up)  6.2 us
    dot_general x1, matrix products, on_device(): along_r2 = jnp.einsum('acij,kj->acik', section, kinetic, precision=highest)  5.87 us
  transfers between devices with their start and end apart: 4, of which 2 were waited for; matrix products, arithmetic and copies ran while one was open for 38% of the time, Pallas kernels for 0%

commit v1 on v0

--- a/solution.py
+++ b/solution.py
@@ -2,6 +2,22 @@
 import jax.numpy as jnp
 from jax import lax
 from jax.sharding import PartitionSpec as P
+
+
+def swapped_with_each(array, axis, split, join):
+    ways, here = (lax.axis_size(axis), lax.axis_index(axis))
+    width = array.shape[split] // ways
+    shape = list(array.shape)
+    shape[split] = width
+    height = shape[join]
+    shape[join] = height * ways
+    full = jnp.zeros(shape, array.dtype)
+    for mask in range(ways):
+        part = lax.dynamic_slice_in_dim(array, (here ^ mask) * width, width, axis=split)
+        if mask:
+            part = lax.ppermute(part, axis, [(d, d ^ mask) for d in range(ways)])
+        full = lax.dynamic_update_slice_in_dim(full, part, (here ^ mask) * height, axis=join)
+    return full
 
 
 def extended(array, sides, width):
@@ -62,9 +78,7 @@
         power = power * ratio
     mixed = jnp.einsum("cd,adq->acq", dipole, block, preferred_element_type=jnp.float32)
     total = total + (field_amp[0] * (row_r + col_r))[None, None, :] * mixed
-    coupled = lax.all_to_all(
-        total.astype(jnp.bfloat16), "chan", split_axis=1, concat_axis=2, tiled=True
-    )
+    coupled = swapped_with_each(total.astype(jnp.bfloat16), "chan", 1, 2)
     coupled = coupled.reshape(coupled.shape[0], local_chan, rows, width)
     ham = along_r1 + along_r2 + potential[None] * section + coupled.astype(jnp.float32)
     return jnp.stack([ham[1], -ham[0]])

time: 112 us -> 108 us (0.964)
  waiting for transfers between devices: 38.1 us -> 32.3 us
  local copies, waits for them, and re-layouts: 26.3 us -> 29.8 us
  starting transfers between devices: 15.6 us -> 12.9 us
  other arithmetic: 5.95 us -> 8.39 us
  matrix products: 24.4 us -> 22.6 us
    ppermute x0 -> x3, waiting for transfers between devices: none -> 16.4 us  [swapped_with_each(): part = lax.ppermute(part, axis, [(d, d ^ mask) for d in range(ways)])]
    all_to_all x1 -> x0, waiting for transfers between devices: 13.5 us -> none  [on_device(): lax.all_to_all(total.astype(jnp.bfloat16), 'chan', split_axis=1, concat_a...]
    convert_element_type x3 -> x0, local copies, waits for them, and re-layouts: 11.8 us -> none  [the longest x2 8.79 us: on_device(): coupled.astype(jnp.float32)]
    all_to_all x1, waiting for transfers between devices: 24.7 us -> 16 us  [on_device(): lax.all_to_all(sent, 'chan', split_axis=2, concat_axis=1, tiled=True)]
    dynamic_update_slice x0 -> x4, local copies, waits for them, and re-layouts: none -> 5.73 us  [swapped_with_each(): lax.dynamic_update_slice_in_dim(full, part, (here ^ mask) * height, axis=...]
    all_to_all x1 -> x0, starting transfers between devices: 4.54 us -> none  [on_device(): lax.all_to_all(total.astype(jnp.bfloat16), 'chan', split_axis=1, concat_a...]
    ppermute x0 -> x3, local copies, waits for them, and re-layouts: none -> 4.46 us  [swapped_with_each(): part = lax.ppermute(part, axis, [(d, d ^ mask) for d in range(ways)])]
    dynamic_slice x0 -> x2, local copies, waits for them, and re-layouts: none -> 3.24 us  [swapped_with_each(): lax.dynamic_slice_in_dim(array, (here ^ mask) * width, width, axis=split)]
  transfers between devices with their start and end apart: 4 -> 6, of which waited for: 2 -> 3; matrix products, arithmetic and copies ran while one was open for 38% -> 46% of each run, Pallas kernels for 0% -> 0%
where the time goes in v1:
time: 108 us; the launch traced here: 107 us
  waiting for transfers between devices  32.3 us (30%)
  local copies, waits for them, and re-layouts  29.8 us (28%)
  matrix products  22.6 us (21%)
  starting transfers between devices  12.9 us (12%)
  other arithmetic  8.39 us (8%)
    ppermute x3, waiting for transfers between devices, swapped_with_each(): part = lax.ppermute(part, axis, [(d, d ^ mask) for d in range(ways)])  16.4 us
    all_to_all x1, waiting for transfers between devices, on_device(): lax.all_to_all(sent, 'chan', split_axis=2, concat_axis=1, tiled=True)  16 us
    dot_general x4, matrix products, on_device(): jnp.einsum('cd,adq->acq', gaunt[order], block, preferred_element_type=jnp...  8.34 us
    all_to_all x2, local copies, waits for them, and re-layouts, on_device(): lax.all_to_all(sent, 'chan', split_axis=2, concat_axis=1, tiled=True)  6.62 us
    ppermute x1, starting transfers between devices, extended(): before = lax.ppermute(last, axis, up)  6.18 us
    dot_general x1, matrix products, on_device(): along_r2 = jnp.einsum('acij,kj->acik', section, kinetic, precision=highest)  5.85 us
    dynamic_update_slice x4, local copies, waits for them, and re-layouts, swapped_with_each(): lax.dynamic_update_slice_in_dim(full, part, (here ^ mask) * height, axis=...  5.73 us
    dot_general x1, matrix products, on_device(): jnp.einsum('ij,acjk->acik', local_band, padded, precision=highest)  5.53 us
  transfers between devices with their start and end apart: 6, of which 3 were waited for; matrix products, arithmetic and copies ran while one was open for 46% of the time, Pallas kernels for 0%

profile of v1, /device:TPU:0, one launch (start us, length us, event | category | flops | bytes accessed | tf_op | source)
XLA Modules:
  0.0 107.0 jit_solution(7406131078511785897)
XLA Ops:
  0.0 4.5 %fusion.43 = bf16[2,192,16,128]{3,2,1,0:T(8,128)(2,1)} fusion(f32[2,192,16,128]{3,2,1,0:T(8,128)} %param.7, f32[2,192,16,128]{3,2,1,0:T(8,128)} %param.8), kind=kLoop, calls=%fused_computation.76 | loop fusion | flops 2359296 | bytes 7864320 | tf_op jit(solution)/shard_map/convert_element_type | solution.py:48
  4.5 6.2 %collective-permute-start = (bf16[2,192,16,128]{3,2,1,0:T(8,128)(2,1)}, bf16[2,192,16,128]{3,2,1,0:T(8,128)(2,1)}, u32[]{:S(2)}, u32[]{:S(2)}) collective-permute-start(bf16[2,192,16,128]{3,2,1,0:T(8,128)(2,1)} %fusion.43), channel_id=1, source_target_pairs={{0,1},{1,2},{2,3},{3,4},{4,5},{5,6},{6,7},{8,9},{9,10},{10,11},{11... | collective-permute-start | bytes 4718600 | tf_op jit(solution)/shard_map/ppermute | solution.py:30
  12.0 4.7 %copy.51 = bf16[2,192,16,128]{1,0,3,2:T(2,128)(2,1)} copy(bf16[2,192,16,128]{3,2,1,0:T(8,128)(2,1)} %fusion.43) | data formatting | bytes 3145728 | tf_op jit(solution)/shard_map/reshape | solution.py:62
  16.7 3.6 %all-to-all-start = ((bf16[2,192,2048]{1,0,2:T(2,128)(2,1)}), bf16[2,192,2048]{1,0,2:T(2,128)(2,1)S(1)}, u32[]{:S(2)}, u32[]{:S(2)}) async-start(bf16[2,192,2048]{1,0,2:T(2,128)(2,1)} %bitcast.65), calls=%async_computation | async-start | bytes 4194304 | tf_op jit(solution)/shard_map/all_to_all | solution.py:64
  24.2 5.8 %fusion.22 = f32[2,192,16,128]{3,2,1,0:T(8,128)} fusion(f32[128,128]{1,0:T(8,128)S(1)} %copy-done.3, f32[2,192,16,128]{3,2,1,0:T(8,128)} %param.7, f32[2,192,16,128]{3,2,1,0:T(8,128)} %param.8), kind=kOutput, calls=%fused_computation.31 | convolution fusion | flops 1209532416 | bytes 9502720 | tf_op jit(solution)/shard_map/acij,kj->acik/dot_general | solution.py:47
  30.0 16.0 %all-to-all-done = bf16[2,192,2048]{1,0,2:T(2,128)(2,1)S(1)} async-done(((bf16[2,192,2048]{1,0,2:T(2,128)(2,1)}), bf16[2,192,2048]{1,0,2:T(2,128)(2,1)S(1)}, u32[]{:S(2)}, u32[]{:S(2)}) %all-to-all-start) | async-done | bytes 1572896 | tf_op jit(solution)/shard_map/all_to_all | solution.py:64
  46.0 4.8 %copy.52 = bf16[2,192,4,512]{3,2,1,0:T(4,128)(2,1)} copy(bf16[2,192,4,512]{1,0,3,2:T(2,128)(2,1)S(1)} %bitcast.64) | data formatting | bytes 3145728 | tf_op jit(solution)/shard_map/all_to_all | solution.py:64
  50.7 1.9 %copy.34 = bf16[2,4,192,512]{3,2,1,0:T(8,128)(2,1)S(1)} copy(bf16[2,4,192,512]{3,1,2,0:T(4,128)(2,1)} %bitcast.66) | data formatting | bytes 3145728 | tf_op jit(solution)/shard_map/all_to_all | solution.py:64
  52.6 2.8 %fusion.10 = f32[2,512,768]{2,1,0:T(8,128)S(1)} fusion(bf16[2,768,512]{2,1,0:T(8,128)(2,1)S(1)} %bitcast.67, bf16[4,768,768]{2,1,0:T(8,128)(2,1)} %param.9), kind=kOutput, calls=%fused_computation.15 | convolution fusion | flops 1207959552 | bytes 5898240 | tf_op jit(solution)/shard_map/cd,adq->acq/dot_general | solution.py:76
  55.4 2.7 %fusion.12 = f32[2,512,768]{2,1,0:T(8,128)S(1)} fusion(bf16[2,768,512]{2,1,0:T(8,128)(2,1)S(1)} %bitcast.68, bf16[4,768,768]{2,1,0:T(8,128)(2,1)} %param.9), kind=kOutput, calls=%fused_computation.17 | convolution fusion | flops 1207959552 | bytes 5898240 | tf_op jit(solution)/shard_map/cd,adq->acq/dot_general | solution.py:76
  58.1 1.4 %fusion.14 = f32[2,512,768]{2,1,0:T(8,128)S(1)} fusion(bf16[2,768,512]{2,1,0:T(8,128)(2,1)S(1)} %bitcast.69, bf16[4,768,768]{2,1,0:T(8,128)(2,1)S(1)} %bitcast.75), kind=kOutput, calls=%fused_computation.19 | convolution fusion | flops 1207959552 | bytes 5898240 | tf_op jit(solution)/shard_map/cd,adq->acq/dot_general | solution.py:76
  59.6 1.4 %fusion.16 = f32[2,512,768]{2,1,0:T(8,128)S(1)} fusion(bf16[2,768,512]{2,1,0:T(8,128)(2,1)S(1)} %bitcast.70, bf16[4,768,768]{2,1,0:T(8,128)(2,1)S(1)} %bitcast.75), kind=kOutput, calls=%fused_computation.21 | convolution fusion | flops 1207959552 | bytes 5898240 | tf_op jit(solution)/shard_map/cd,adq->acq/dot_general | solution.py:76
  61.1 2.9 %add_convert_fusion = bf16[2,512,768]{2,1,0:T(8,128)(2,1)S(1)} fusion(f32[2,512,768]{2,1,0:T(8,128)S(1)} %fusion.10, f32[2,512,768]{2,1,0:T(8,128)S(1)} %fusion.12, f32[2,512,768]{2,1,0:T(8,128)S(1)} %fusion.14, f32[2,512,768]{2,1,0:T(8,128)S(1)} %fusion.16, bf16[2,768,512]{2,1,0:T(8,128)(2,1)S(1)} %bitcast.71, f32[512]{0:T(512)S(1)} %copy-done.5, ...), kind=kOutput, calls=%fused_computation.10 | convolution fusion | flops 1215823872 | bytes 16918528 | tf_op jit(solution)/shard_map/cd,adq->acq/dot_general | solution.py:79
  64.0 2.3 %dynamic-slice_bitcast_fusion = (bf16[2,192,512]{1,2,0:T(8,128)(2,1)}, bf16[2,192,512]{1,2,0:T(8,128)(2,1)}, bf16[2,192,512]{1,2,0:T(8,128)(2,1)}, bf16[2,192,512]{1,2,0:T(8,128)(2,1)S(1)}) fusion(bf16[2,512,768]{2,1,0:T(8,128)(2,1)S(1)} %add_convert_fusion, s32[]{:T(128)S(6)} %select_n.84, s32[]{:T(128)S(6)} %select_n.82, s32[]{:T(128)S(6)} %select_n.80, ...), kind=kLoop, calls=%fused_computation.27 | loop fusion | bytes 3145744 | tf_op jit(solution)/shard_map/dynamic_slice | solution.py:16
  66.6 1.5 %collective-permute-start.4 = (bf16[2,192,512]{1,2,0:T(8,128)(2,1)}, bf16[2,192,512]{1,2,0:T(8,128)(2,1)}, u32[]{:S(2)}, u32[]{:S(2)}) collective-permute-start(bf16[2,192,512]{1,2,0:T(8,128)(2,1)} %get-tuple-element.7), channel_id=1, source_target_pairs={{0,24},{8,16},{16,8},{24,0},{1,25},{9,17},{17,9},{25,1},{2,26},{10... | collective-permute-start | bytes 1179656 | tf_op jit(solution)/shard_map/ppermute | solution.py:18
  69.6 1.4 %broadcast_in_dim.2 = bf16[2,192,2048]{2,1,0:T(8,128)(2,1)} broadcast(bf16[]{:T(256)} %constant.83.clone.1), dimensions={} | broadcast | bytes 1572866 | tf_op jit(solution)/shard_map/broadcast_in_dim | solution.py:14
  71.0 1.8 %constant_dynamic-update-slice_fusion.3 = bf16[2,192,2048]{2,1,0:T(8,128)(2,1)} fusion(bf16[2,192,2048]{2,1,0:T(8,128)(2,1)} %broadcast_in_dim.2, bf16[2,192,512]{2,1,0:T(8,128)(2,1)} %copy.40, s32[]{:T(128)S(6)} %select_n.79), kind=kLoop, calls=%fused_computation.45 | loop fusion | bytes 786436 | tf_op jit(solution)/shard_map/dynamic_update_slice | solution.py:19
  74.0 7.3 %collective-permute-done.3 = bf16[2,192,512]{1,2,0:T(8,128)(2,1)} collective-permute-done((bf16[2,192,512]{1,2,0:T(8,128)(2,1)}, bf16[2,192,512]{1,2,0:T(8,128)(2,1)}, u32[]{:S(2)}, u32[]{:S(2)}) %collective-permute-start.3) | collective-permute-done | bytes 393248 | tf_op jit(solution)/shard_map/ppermute | solution.py:18
  82.6 9.1 %collective-permute-done.4 = bf16[2,192,512]{1,2,0:T(8,128)(2,1)} collective-permute-done((bf16[2,192,512]{1,2,0:T(8,128)(2,1)}, bf16[2,192,512]{1,2,0:T(8,128)(2,1)}, u32[]{:S(2)}, u32[]{:S(2)}) %collective-permute-start.4) | collective-permute-done | bytes 393248 | tf_op jit(solution)/shard_map/ppermute | solution.py:18
  91.6 2.0 %copy.43 = bf16[2,192,512]{2,1,0:T(8,128)(2,1)} copy(bf16[2,192,512]{1,2,0:T(8,128)(2,1)} %collective-permute-done.4) | data formatting | bytes 786432 | tf_op jit(solution)/shard_map/ppermute | solution.py:18
  95.3 2.3 %constant_dynamic-update-slice_fusion = bf16[2,192,2048]{2,1,0:T(8,128)(2,1)} fusion(bf16[2,192,2048]{2,1,0:T(8,128)(2,1)} %constant_dynamic-update-slice_fusion.1, bf16[2,192,512]{2,1,0:T(8,128)(2,1)} %copy.43, s32[]{:T(128)S(6)} %select_n.85), kind=kLoop, calls=%fused_computation.42 | loop fusion | bytes 786436 | tf_op jit(solution)/shard_map/dynamic_update_slice | solution.py:19
  97.6 1.8 %copy.53 = f32[48,8,16,128]{3,2,1,0:T(8,128)S(1)} copy(bf16[48,8,16,128]{3,1,2,0:T(8,128)(2,1)} %bitcast.55) | data formatting | bytes 4718592
  99.5 5.5 %bitcast_add_fusion = f32[2,192,16,128]{3,2,1,0:T(8,128)S(1)} fusion(f32[2,192,16,128]{3,2,1,0:T(8,128)} %fusion.22, bf16[2,192,16,128]{3,2,1,0:T(8,128)(2,1)} %collective-permute-done.1, bf16[2,192,16,128]{3,2,1,0:T(8,128)(2,1)} %fusion.43, bf16[2,192,16,128]{3,2,1,0:T(8,128)(2,1)} %collective-permute-done, f32[192,16,128]{2,1,0:T(8,128)S(1)} %subtract_subtract_fusion, ...), kind=kOutput, calls=%fused_computation.6 | convolution fusion | flops 471859200 | bytes 22028292 | tf_op jit(solution)/shard_map/ij,acjk->acik/dot_general | solution.py:52
  105.3 1.7 %copy-done.10 = f32[2,192,16,128]{3,2,1,0:T(8,128)} copy-done((f32[2,192,16,128]{3,2,1,0:T(8,128)}, f32[2,192,16,128]{3,2,1,0:T(8,128)S(1)}, u32[]{:S(2)}) %copy-start.10) | copy-done | bytes 3145752
  (54 shorter events, 10.7 us)
Async XLA Ops:
  0.0 61.0 %copy-start = (bf16[768,768]{1,0:T(8,128)(2,1)S(1)}, bf16[768,768]{1,0:T(8,128)(2,1)}, u32[]{:S(2)}) copy-start(bf16[768,768]{1,0:T(8,128)(2,1)} %param.10) | copy-start | bytes 3538948
  4.5 18.2 %copy-start.7 = (s32[192,2]{0,1:T(2,128)S(1)}, s32[192,2]{0,1:T(2,128)}, u32[]{:S(2)}) copy-start(s32[192,2]{0,1:T(2,128)} %param.12) | copy-start | bytes 4612
  4.5 18.3 %copy-start.3 = (f32[128,128]{1,0:T(8,128)S(1)}, f32[128,128]{1,0:T(8,128)}, u32[]{:S(2)}) copy-start(f32[128,128]{1,0:T(8,128)} %param.11) | copy-start | bytes 196612
  4.5 94.9 %collective-permute-start = (bf16[2,192,16,128]{3,2,1,0:T(8,128)(2,1)}, bf16[2,192,16,128]{3,2,1,0:T(8,128)(2,1)}, u32[]{:S(2)}, u32[]{:S(2)}) collective-permute-start(bf16[2,192,16,128]{3,2,1,0:T(8,128)(2,1)} %fusion.43), channel_id=1, source_target_pairs={{0,1},{1,2},{2,3},{3,4},{4,5},{5,6},{6,7},{8,9},{9,10},{10,11},{11... | collective-permute-start | bytes 4718600 | tf_op jit(solution)/shard_map/ppermute | solution.py:30
  10.7 88.7 %collective-permute-start.1 = (bf16[2,192,16,128]{3,2,1,0:T(8,128)(2,1)}, bf16[2,192,16,128]{3,2,1,0:T(8,128)(2,1)}, u32[]{:S(2)}, u32[]{:S(2)}) collective-permute-start(bf16[2,192,16,128]{3,2,1,0:T(8,128)(2,1)} %fusion.43), channel_id=1, source_target_pairs={{1,0},{2,1},{3,2},{4,3},{5,4},{6,5},{7,6},{9,8},{10,9},{11,10},{12... | collective-permute-start | bytes 4718600 | tf_op jit(solution)/shard_map/ppermute | solution.py:31
  16.7 29.2 %all-to-all-start = ((bf16[2,192,2048]{1,0,2:T(2,128)(2,1)}), bf16[2,192,2048]{1,0,2:T(2,128)(2,1)S(1)}, u32[]{:S(2)}, u32[]{:S(2)}) async-start(bf16[2,192,2048]{1,0,2:T(2,128)(2,1)} %bitcast.65), calls=%async_computation | async-start | bytes 4194304 | tf_op jit(solution)/shard_map/all_to_all | solution.py:64
  50.7 7.4 %slice-start = ((s8[4718592]{0:T(1024)(128)(4,1)}), s8[4194304]{0:T(1024)(128)(4,1)S(1)}, s32[]{:S(2)}) async-start(s8[4718592]{0:T(1024)(128)(4,1)} %bitcast.74), calls=%async_computation.1 | async-start | bytes 8388608
  52.6 5.5 %slice-start.1 = ((s8[4718592]{0:T(1024)(128)(4,1)}), s8[524288]{0:T(1024)(128)(4,1)S(1)}, s32[]{:S(2)}) async-start(s8[4718592]{0:T(1024)(128)(4,1)} %bitcast.74), calls=%async_computation.2 | async-start | bytes 1048576
  59.6 1.5 %copy-start.4 = (f32[512]{0:T(512)S(1)}, f32[512]{0:T(512)}, u32[]{:S(2)}) copy-start(f32[512]{0:T(512)} %fusion.39) | copy-start | bytes 6148
  59.6 1.5 %copy-start.5 = (f32[512]{0:T(512)S(1)}, f32[512]{0:T(512)}, u32[]{:S(2)}) copy-start(f32[512]{0:T(512)} %get-tuple-element.13) | copy-start | bytes 6148
  59.6 1.5 %copy-start.6 = (f32[512]{0:T(512)S(1)}, f32[512]{0:T(512)}, u32[]{:S(2)}) copy-start(f32[512]{0:T(512)} %get-tuple-element.14) | copy-start | bytes 6148
  63.9 4.1 %copy-start.8 = (f32[16]{0:T(128)S(1)}, f32[16]{0:T(128)}, u32[]{:S(2)}) copy-start(f32[16]{0:T(128)} %broadcast_divide_fusion.2) | copy-start | bytes 196
  66.2 6.6 %collective-permute-start.2 = (bf16[2,192,512]{1,2,0:T(8,128)(2,1)}, bf16[2,192,512]{1,2,0:T(8,128)(2,1)}, u32[]{:S(2)}, u32[]{:S(2)}) collective-permute-start(bf16[2,192,512]{1,2,0:T(8,128)(2,1)} %get-tuple-element.9), channel_id=1, source_target_pairs={{0,8},{8,0},{16,24},{24,16},{1,9},{9,1},{17,25},{25,17},{2,10},{10... | collective-permute-start | bytes 1179656 | tf_op jit(solution)/shard_map/ppermute | solution.py:18
  66.2 15.1 %collective-permute-start.3 = (bf16[2,192,512]{1,2,0:T(8,128)(2,1)}, bf16[2,192,512]{1,2,0:T(8,128)(2,1)}, u32[]{:S(2)}, u32[]{:S(2)}) collective-permute-start(bf16[2,192,512]{1,2,0:T(8,128)(2,1)} %get-tuple-element.8), channel_id=1, source_target_pairs={{0,16},{8,24},{16,0},{24,8},{1,17},{9,25},{17,1},{25,9},{2,18},{10... | collective-permute-start | bytes 1179656 | tf_op jit(solution)/shard_map/ppermute | solution.py:18
  66.6 25.0 %collective-permute-start.4 = (bf16[2,192,512]{1,2,0:T(8,128)(2,1)}, bf16[2,192,512]{1,2,0:T(8,128)(2,1)}, u32[]{:S(2)}, u32[]{:S(2)}) collective-permute-start(bf16[2,192,512]{1,2,0:T(8,128)(2,1)} %get-tuple-element.7), channel_id=1, source_target_pairs={{0,24},{8,16},{16,8},{24,0},{1,25},{9,17},{17,9},{25,1},{2,26},{10... | collective-permute-start | bytes 1179656 | tf_op jit(solution)/shard_map/ppermute | solution.py:18
  94.4 5.0 %copy-start.1 = (f32[2,192,16,128]{3,2,1,0:T(8,128)S(1)}, f32[2,192,16,128]{3,2,1,0:T(8,128)}, u32[]{:S(2)}) copy-start(f32[2,192,16,128]{3,2,1,0:T(8,128)} %param.7) | copy-start | bytes 9437188
  94.4 5.0 %copy-start.2 = (f32[2,192,16,128]{3,2,1,0:T(8,128)S(1)}, f32[2,192,16,128]{3,2,1,0:T(8,128)}, u32[]{:S(2)}) copy-start(f32[2,192,16,128]{3,2,1,0:T(8,128)} %param.8) | copy-start | bytes 9437188
  99.4 5.6 %copy-start.9 = (f32[2,192,16,128]{3,2,1,0:T(8,128)S(1)}, f32[2,192,16,128]{3,2,1,0:T(8,128)}, u32[]{:S(2)}) copy-start(f32[2,192,16,128]{3,2,1,0:T(8,128)} %custom-call) | copy-start | bytes 9437188
  105.3 1.7 %copy-start.10 = (f32[2,192,16,128]{3,2,1,0:T(8,128)}, f32[2,192,16,128]{3,2,1,0:T(8,128)S(1)}, u32[]{:S(2)}) copy-start(f32[2,192,16,128]{3,2,1,0:T(8,128)S(1)} %get-tuple-element.21) | copy-start | bytes 9437188
